TPU v7x, 32 devices: a whole 2x2x4 slice. The times are simulated.
32 devices in a mesh: pipe: 2 (over x), expert: 16 (over z, y, core).
Axes of the slice: x: 2, y: 2, z: 4, core: 2. Of those that a mesh axis runs over, the one named last changes fastest.
Arguments:
- front_tokens: bfloat16 [2, 192, 3584], P('pipe', 'expert'), may hold values from -6 to 6
- front_routes: int32 [2, 192, 2], P('pipe', 'expert'), may hold values from 0 to 1, all different within a row; in each aligned block of 12 rows (0 to 11, 12 to 23, ..., all dimensions but the last counted through in order) at most 12 rows name the same one
- front_mixing: int32 [2, 192, 2], P('pipe', 'expert'), may hold values from 1 to 15
- back_tokens: bfloat16 [2, 192, 3584], P('pipe', 'expert'), may hold values from -6 to 6
- back_routes: int32 [2, 192, 2], P('pipe', 'expert'), may hold values from 0 to 1, all different within a row; in each aligned block of 12 rows (0 to 11, 12 to 23, ..., all dimensions but the last counted through in order) at most 12 rows name the same one
- back_mixing: int32 [2, 192, 2], P('pipe', 'expert'), may hold values from 1 to 15
- back_upstream: bfloat16 [2, 192, 3584], P('pipe', 'expert'), may hold values from -6 to 6
- gate_weight: bfloat16 [2, 3584, 2048], P('pipe', None, 'expert'), may hold values from -0.09375 to 0.09375
- up_weight: bfloat16 [2, 3584, 2048], P('pipe', None, 'expert'), may hold values from -0.09375 to 0.09375
- down_weight: bfloat16 [2, 2048, 3584], P('pipe', 'expert'), may hold values from -0.1875 to 0.1875
Outputs:
- front_result: bfloat16 [2, 192, 3584], P('pipe', 'expert')
- token_grads: bfloat16 [2, 192, 3584], P('pipe', 'expert')
- gate_grads: bfloat16 [2, 1792, 2048], P('pipe', None, 'expert')
- up_grads: bfloat16 [2, 1792, 2048], P('pipe', None, 'expert')
- down_grads: bfloat16 [2, 2048, 1792], P('pipe', 'expert')
Inputs may be any that keep to these rules, and one draw needn't show every extreme that they name: `front_routes`: each row names 2 different experts; within each device's block of 12 rows no expert is named more than 12 times, a bound that some block reaches. `back_routes`: each row names 2 different experts; within each device's block of 12 rows no expert is named more than 12 times, a bound that some block reaches.
All inputs are finite; a program needn't handle non-finite values.
Results may differ from a plain program's by a relative error of at most 0.0071.
Values may be sent and summed in bfloat16 or wider, within the bound.
A program may use at most 64 MiB of HBM per device.

v0:
```python
import jax
import jax.numpy as jnp
from jax import lax
from jax.sharding import PartitionSpec as P

SHARDS = 8
weight_unit = 0.0625


def hit_tables(routes, mixing, experts, capacity):
    token_count, route_count = routes.shape
    flat_routes = routes.reshape(token_count * route_count)
    matches = (flat_routes[:, None] == jnp.arange(experts, dtype=jnp.int32)[None, :]).astype(
        jnp.int32
    )
    earlier = jnp.cumsum(matches, axis=0) - matches
    position = jnp.sum(earlier * matches, axis=1)
    slot_ids = flat_routes * capacity + position
    hit_table = (
        slot_ids[:, None] == jnp.arange(experts * capacity, dtype=jnp.int32)[None, :]
    ).astype(jnp.float32)
    hit_table = hit_table.reshape(token_count, route_count, experts * capacity)
    weights = mixing.astype(jnp.float32) * weight_unit
    picker = jnp.sum(hit_table, axis=1)
    mix_table = jnp.sum(hit_table * weights[:, :, None], axis=1)
    return (picker, mix_table)


def deliver(slot_rows, experts, capacity):
    stacks = slot_rows.shape[0]
    feature_count = slot_rows.shape[2]
    copies = jnp.repeat(slot_rows.reshape(stacks, experts, capacity, feature_count), SHARDS, axis=1)
    landed = lax.all_to_all(copies, "expert", split_axis=1, concat_axis=1, tiled=True)
    return landed.reshape(stacks, experts * SHARDS * capacity, feature_count)


def collect(shard_parts, experts, capacity):
    feature_count = shard_parts.shape[1]
    sources = experts * SHARDS
    returned = lax.all_to_all(
        shard_parts.reshape(sources, capacity, feature_count),
        "expert",
        split_axis=0,
        concat_axis=0,
        tiled=True,
    )
    summed = jnp.sum(
        returned.reshape(experts, SHARDS, capacity, feature_count).astype(jnp.float32), axis=1
    )
    result_rows = summed.astype(jnp.bfloat16).reshape(experts * capacity, feature_count)
    return result_rows


def mirror_move(values, split_dim, concat_dim):
    return lax.all_to_all(values, "pipe", split_axis=split_dim, concat_axis=concat_dim, tiled=True)


def local(
    front_tokens,
    front_routes,
    front_mixing,
    back_tokens,
    back_routes,
    back_mixing,
    back_upstream,
    gate_weight,
    up_weight,
    down_weight,
):
    experts = lax.axis_size("expert") // SHARDS
    token_count = front_tokens.shape[1]
    route_count = front_routes.shape[2]
    feature_count = front_tokens.shape[2]
    capacity = min(token_count, max(2, 3 * token_count * route_count // (2 * experts)))
    front_pick, front_mix = hit_tables(front_routes[0], front_mixing[0], experts, capacity)
    back_pick, back_mix = hit_tables(back_routes[0], back_mixing[0], experts, capacity)
    front_slots = jnp.dot(
        front_pick.T.astype(jnp.bfloat16), front_tokens[0], preferred_element_type=jnp.float32
    ).astype(jnp.bfloat16)
    back_slots = jnp.dot(
        back_pick.T.astype(jnp.bfloat16), back_tokens[0], preferred_element_type=jnp.float32
    ).astype(jnp.bfloat16)
    scaled_slots = jnp.dot(
        back_mix.T, back_upstream[0].astype(jnp.float32), precision=lax.Precision.HIGHEST
    ).astype(jnp.bfloat16)
    landed = deliver(jnp.stack([front_slots, back_slots, scaled_slots]), experts, capacity)
    gate_cols = gate_weight[0]
    up_cols = up_weight[0]
    down_rows = down_weight[0]
    front_rows = landed[0]
    front_gate = jnp.dot(front_rows, gate_cols, preferred_element_type=jnp.float32)
    front_up = jnp.dot(front_rows, up_cols, preferred_element_type=jnp.float32)
    front_hidden = (jax.nn.silu(front_gate) * front_up).astype(jnp.bfloat16)
    front_parts = jnp.dot(front_hidden, down_rows, preferred_element_type=jnp.float32).astype(
        jnp.bfloat16
    )
    front_summed = collect(front_parts, experts, capacity)
    front_result = jnp.dot(
        front_mix, front_summed.astype(jnp.float32), precision=lax.Precision.HIGHEST
    ).astype(jnp.bfloat16)
    back_rows = landed[1]
    scaled_rows = landed[2]
    back_gate = jnp.dot(back_rows, gate_cols, preferred_element_type=jnp.float32)
    back_up = jnp.dot(back_rows, up_cols, preferred_element_type=jnp.float32)
    gate_act = jax.nn.silu(back_gate)
    gate_sig = jax.nn.sigmoid(back_gate)
    back_hidden = (gate_act * back_up).astype(jnp.bfloat16)
    down_section = jnp.dot(scaled_rows.T, back_hidden, preferred_element_type=jnp.float32).astype(
        jnp.bfloat16
    )
    hidden_grad = jnp.dot(scaled_rows, down_rows.T, preferred_element_type=jnp.float32)
    act_slope = gate_sig * (1.0 + back_gate * (1.0 - gate_sig))
    gate_delta = (hidden_grad * back_up * act_slope).astype(jnp.bfloat16)
    up_delta = (hidden_grad * gate_act).astype(jnp.bfloat16)
    gate_section = jnp.dot(back_rows.T, gate_delta, preferred_element_type=jnp.float32).astype(
        jnp.bfloat16
    )
    up_section = jnp.dot(back_rows.T, up_delta, preferred_element_type=jnp.float32).astype(
        jnp.bfloat16
    )
    back_parts = (
        jnp.dot(gate_delta, gate_cols.T, preferred_element_type=jnp.float32)
        + jnp.dot(up_delta, up_cols.T, preferred_element_type=jnp.float32)
    ).astype(jnp.bfloat16)
    grad_slots = collect(back_parts, experts, capacity)
    token_grads = jnp.dot(
        back_pick.astype(jnp.bfloat16), grad_slots, preferred_element_type=jnp.float32
    ).astype(jnp.bfloat16)
    section_grads = lax.optimization_barrier(jnp.stack([gate_section, up_section, down_section]))
    pipe_count = lax.axis_size("pipe")
    half_rows = feature_count // 2
    upper_half = lax.axis_index("pipe") * 2 >= pipe_count
    own_half = jnp.where(upper_half, section_grads[:, half_rows:], section_grads[:, :half_rows])
    leaving = jnp.where(upper_half, section_grads[:, :half_rows], section_grads[:, half_rows:])
    piece_rows = half_rows // pipe_count
    spread_out = mirror_move(leaving, 1, 0)
    by_source = spread_out.reshape(pipe_count, 3, piece_rows, leaving.shape[2])
    reversed_sources = jnp.flip(by_source, axis=0).reshape(
        pipe_count * 3, piece_rows, leaving.shape[2]
    )
    leaving = mirror_move(reversed_sources, 0, 1)
    summed = (own_half.astype(jnp.float32) + leaving.astype(jnp.float32)).astype(jnp.bfloat16)
    return (
        front_result[None],
        token_grads[None],
        summed[0][None],
        summed[1][None],
        summed[2].T[None],
    )


def solution(mesh):
    placed = (
        P("pipe", "expert", None),
        P("pipe", "expert", None),
        P("pipe", "expert", None),
        P("pipe", "expert", None),
        P("pipe", "expert", None),
        P("pipe", "expert", None),
        P("pipe", "expert", None),
        P("pipe", None, "expert"),
        P("pipe", None, "expert"),
        P("pipe", "expert", None),
    )
    return jax.shard_map(
        local,
        mesh=mesh,
        in_specs=placed,
        out_specs=(
            P("pipe", "expert", None),
            P("pipe", "expert", None),
            P("pipe", None, "expert"),
            P("pipe", None, "expert"),
            P("pipe", "expert", None),
        ),
        check_vma=False,
    )
```

profile of v0, /device:TPU:13, one launch (start us, length us, event | category | flops | bytes accessed | tf_op | source)
XLA Modules:
  0.0 313.1 jit_solution(14618682792077326766)
XLA Ops:
  0.7 0.9 copy.61
  1.5 0.1 eq.58
  1.7 0.2 select_reduce_fusion.3
  2.0 0.1 copy.62
  2.1 0.7 bitcast_add_fusion.2
  2.8 0.1 copy.63
  2.9 0.7 multiply_bitcast_fusion.1
  3.6 0.1 copy.64
  3.7 0.8 copy.65
  4.6 0.2 select_reduce_fusion.1
  4.9 0.1 copy.66
  5.0 0.7 bitcast_add_fusion.1
  5.7 0.1 copy.67
  5.8 0.7 multiply_bitcast_fusion
  6.5 0.1 copy.68
  6.6 0.1 convert_reduce_fusion
  6.7 1.2 convolution_convert_fusion.4
  8.0 1.1 convolution_convert_fusion.5
  9.2 0.1 convert_reduce_fusion.1
  9.3 0.2 convolution_convert_fusion.6
  9.6 0.1 pad_maximum_fusion.1
  9.8 3.1 broadcast_in_dim.8
  12.9 6.6 %all-to-all-start = ((bf16[3,16,12,3584]{3,2,0,1:T(8,128)(2,1)}), bf16[3,16,12,3584]{3,2,0,1:T(8,128)(2,1)}, u32[]{:S(2)}, u32[]{:S(2)}) async-start(bf16[3,16,12,3584]{3,2,0,1:T(8,128)(2,1)} %bitcast.97), calls=%async_computation | async-start | bytes 11010048 | tf_op jit(solution)/shard_map/all_to_all | solution.py:33
  19.4 120.6 %all-to-all-done = bf16[3,16,12,3584]{3,2,0,1:T(8,128)(2,1)} async-done(((bf16[3,16,12,3584]{3,2,0,1:T(8,128)(2,1)}), bf16[3,16,12,3584]{3,2,0,1:T(8,128)(2,1)}, u32[]{:S(2)}, u32[]{:S(2)}) %all-to-all-start) | async-done | bytes 4128800 | tf_op jit(solution)/shard_map/all_to_all | solution.py:33
  140.0 5.2 %fusion.40 = (bf16[1,16,12,3584]{3,2,0,1:T(8,128)(2,1)}, bf16[1,16,12,3584]{3,2,0,1:T(8,128)(2,1)}, bf16[1,16,12,3584]{3,2,0,1:T(8,128)(2,1)}) fusion(bf16[3,16,12,3584]{3,2,0,1:T(8,128)(2,1)} %all-to-all-done), kind=kLoop, calls=%fused_computation.75 | loop fusion | bytes 8257536 | tf_op jit(solution)/shard_map/slice | solution.py:102
  145.2 2.4 squeeze.40
  147.6 0.5 fusion.18
  148.1 0.5 fusion.12
  148.7 3.4 %squeeze.39 = bf16[192,3584]{1,0:T(8,128)(2,1)} reshape(bf16[1,16,12,3584]{3,2,0,1:T(8,128)(2,1)} %get-tuple-element.34) | data formatting | bytes 2752512 | tf_op jit(solution)/shard_map/squeeze | solution.py:102
  152.1 2.2 fusion.3
  154.3 0.5 multiply_convert_fusion.1
  154.8 0.7 fusion.2
  155.5 0.7 fusion.1
  156.3 0.3 pad_maximum_fusion
  156.6 0.1 broadcast_select_fusion
  156.7 1.4 copy-done.1
  158.1 8.5 %copy.70 = bf16[3,1792,128]{2,0,1:T(4,128)(2,1)S(1)} copy(bf16[3,1792,128]{2,1,0:T(8,128)(2,1)S(1)} %broadcast_select_fusion) | data formatting | bytes 2752512 | tf_op jit(solution)/shard_map/jit(_where)/select_n | solution.py:134
  166.6 24.4 %all_to_all.39 = bf16[3,1792,128]{2,0,1:T(4,128)(2,1)S(1)} all-to-all(bf16[3,1792,128]{2,0,1:T(4,128)(2,1)S(1)} %copy.70), channel_id=1, replica_groups=mesh['pipe'=2,'expert'=16] {'pipe'}, dimensions={1} | all-to-all | bytes 2752512 | tf_op jit(solution)/shard_map/all_to_all | solution.py:55
  191.1 0.2 copy.71
  191.3 1.2 reverse.3
  192.5 2.5 copy.72
  195.0 4.8 %all-to-all-start.4 = ((bf16[6,896,128]{2,1,0:T(8,128)(2,1)}), bf16[6,896,128]{2,1,0:T(8,128)(2,1)}, u32[]{:S(2)}, u32[]{:S(2)}) async-start(bf16[6,896,128]{2,1,0:T(8,128)(2,1)} %bitcast.20), calls=%async_computation.4 | async-start | bytes 2752512 | tf_op jit(solution)/shard_map/all_to_all | solution.py:55
  199.7 2.4 squeeze.35
  202.1 0.5 fusion.20
  202.6 3.2 %convolution_convert_fusion = bf16[192,3584]{1,0:T(8,128)(2,1)} fusion(bf16[192,3584]{1,0:T(8,128)(2,1)S(1)} %squeeze.35, bf16[1,128,3584]{2,1,0:T(8,128)(2,1)} %param.19, bf16[1,3584,128]{2,1,0:T(8,128)(2,1)S(1)} %copy-done, f32[192,128]{1,0:T(8,128)S(1)} %fusion.20), kind=kOutput, calls=%fused_computation.2 | convolution fusion | flops 353157120 | bytes 4685824 | tf_op jit(solution)/shard_map/dot_general | solution.py:94
  205.9 3.3 %reshape.117 = bf16[16,12,3584]{2,1,0:T(8,128)(2,1)} reshape(bf16[192,3584]{1,0:T(8,128)(2,1)} %convolution_convert_fusion) | data formatting | bytes 2752512 | tf_op jit(solution)/shard_map/reshape | solution.py:41
  209.1 6.6 %all-to-all-done.4 = bf16[6,896,128]{2,1,0:T(8,128)(2,1)} async-done(((bf16[6,896,128]{2,1,0:T(8,128)(2,1)}), bf16[6,896,128]{2,1,0:T(8,128)(2,1)}, u32[]{:S(2)}, u32[]{:S(2)}) %all-to-all-start.4) | async-done | bytes 1376288 | tf_op jit(solution)/shard_map/all_to_all | solution.py:55
  215.7 6.7 %all-to-all-start.1 = ((bf16[16,12,3584]{2,1,0:T(8,128)(2,1)}), bf16[16,12,3584]{2,1,0:T(8,128)(2,1)}, u32[]{:S(2)}, u32[]{:S(2)}) async-start(bf16[16,12,3584]{2,1,0:T(8,128)(2,1)} %reshape.117), calls=%async_computation.1 | async-start | bytes 3670016 | tf_op jit(solution)/shard_map/all_to_all | solution.py:40
  222.4 0.5 fusion.16
  222.9 0.5 fusion
  223.5 1.4 reshape.120
  224.9 39.4 %all-to-all-done.1 = bf16[16,12,3584]{2,1,0:T(8,128)(2,1)} async-done(((bf16[16,12,3584]{2,1,0:T(8,128)(2,1)}), bf16[16,12,3584]{2,1,0:T(8,128)(2,1)}, u32[]{:S(2)}, u32[]{:S(2)}) %all-to-all-start.1) | async-done | bytes 1376288 | tf_op jit(solution)/shard_map/all_to_all | solution.py:40
  264.3 4.9 %all-to-all-start.2 = ((bf16[16,12,3584]{2,1,0:T(8,128)(2,1)}), bf16[16,12,3584]{2,1,0:T(8,128)(2,1)S(1)}, u32[]{:S(2)}, u32[]{:S(2)}) async-start(bf16[16,12,3584]{2,1,0:T(8,128)(2,1)} %reshape.120), calls=%async_computation.2 | async-start | bytes 3670016 | tf_op jit(solution)/shard_map/all_to_all | solution.py:40
  269.2 1.5 convert_bitcast_fusion
  270.8 0.2 copy.73
  271.0 1.6 copy-done.2
  272.5 0.4 fusion.6
  273.0 1.0 slice_bitcast_fusion
  274.0 1.0 copy.74
  275.0 1.8 bitcast_reduce_fusion.1
  276.8 34.2 %all-to-all-done.2 = bf16[16,12,3584]{2,1,0:T(8,128)(2,1)S(1)} async-done(((bf16[16,12,3584]{2,1,0:T(8,128)(2,1)}), bf16[16,12,3584]{2,1,0:T(8,128)(2,1)S(1)}, u32[]{:S(2)}, u32[]{:S(2)}) %all-to-all-start.2) | async-done | bytes 1376288 | tf_op jit(solution)/shard_map/all_to_all | solution.py:40
  311.0 0.3 bitcast_reduce_fusion
  311.4 0.8 fusion.5
  312.2 0.9 fusion.4
  (25 shorter events, 0.8 us)
Async XLA Ops:
  0.6 147.5 %copy-start = (bf16[1,3584,128]{2,1,0:T(8,128)(2,1)S(1)}, bf16[1,3584,128]{2,1,0:T(8,128)(2,1)}, u32[]{:S(2)}) copy-start(bf16[1,3584,128]{2,1,0:T(8,128)(2,1)} %param.18) | copy-start | bytes 2752516
  0.6 8.7 %copy-start.6 = (bf16[1,12,3584]{2,1,0:T(8,128)(2,1)S(1)}, bf16[1,12,3584]{2,1,0:T(8,128)(2,1)}, u32[]{:S(2)}) copy-start(bf16[1,12,3584]{2,1,0:T(8,128)(2,1)} %param.10) | copy-start | bytes 258052
  12.9 127.1 %all-to-all-start = ((bf16[3,16,12,3584]{3,2,0,1:T(8,128)(2,1)}), bf16[3,16,12,3584]{3,2,0,1:T(8,128)(2,1)}, u32[]{:S(2)}, u32[]{:S(2)}) async-start(bf16[3,16,12,3584]{3,2,0,1:T(8,128)(2,1)} %bitcast.97), calls=%async_computation | async-start | bytes 11010048 | tf_op jit(solution)/shard_map/all_to_all | solution.py:33
  145.2 2.5 copy-start.3
  152.1 2.2 copy-start.4
  152.1 2.2 copy-start.5
  156.6 1.6 copy-start.1
  195.0 20.8 %all-to-all-start.4 = ((bf16[6,896,128]{2,1,0:T(8,128)(2,1)}), bf16[6,896,128]{2,1,0:T(8,128)(2,1)}, u32[]{:S(2)}, u32[]{:S(2)}) async-start(bf16[6,896,128]{2,1,0:T(8,128)(2,1)} %bitcast.20), calls=%async_computation.4 | async-start | bytes 2752512 | tf_op jit(solution)/shard_map/all_to_all | solution.py:55
  215.7 48.6 %all-to-all-start.1 = ((bf16[16,12,3584]{2,1,0:T(8,128)(2,1)}), bf16[16,12,3584]{2,1,0:T(8,128)(2,1)}, u32[]{:S(2)}, u32[]{:S(2)}) async-start(bf16[16,12,3584]{2,1,0:T(8,128)(2,1)} %reshape.117), calls=%async_computation.1 | async-start | bytes 3670016 | tf_op jit(solution)/shard_map/all_to_all | solution.py:40
  264.3 46.7 %all-to-all-start.2 = ((bf16[16,12,3584]{2,1,0:T(8,128)(2,1)}), bf16[16,12,3584]{2,1,0:T(8,128)(2,1)S(1)}, u32[]{:S(2)}, u32[]{:S(2)}) async-start(bf16[16,12,3584]{2,1,0:T(8,128)(2,1)} %reshape.120), calls=%async_computation.2 | async-start | bytes 3670016 | tf_op jit(solution)/shard_map/all_to_all | solution.py:40
  270.8 1.8 copy-start.2
where the time goes:
time: 314 us; the launch traced here: 313 us
  waiting for transfers between devices  201 us (64%)
  local copies, waits for them, and re-layouts  41.6 us (13%)
  blocking collectives  24.4 us (8%)
  starting transfers between devices  22.9 us (7%)
  matrix products  14.2 us (5%)
  other arithmetic  8.21 us (3%)
    all_to_all x1, waiting for transfers between devices, deliver(): lax.all_to_all(copies, 'expert', split_axis=1, concat_axis=1, tiled=True)  121 us
    all_to_all x2, waiting for transfers between devices, collect(): lax.all_to_all(shard_parts.reshape(sources, capacity, feature_count), 'ex...  73.6 us
    all_to_all x1, blocking collectives, mirror_move(): lax.all_to_all(values, 'pipe', split_axis=split_dim, concat_axis=concat_d...  24.4 us
    all_to_all x2, starting transfers between devices, collect(): lax.all_to_all(shard_parts.reshape(sources, capacity, feature_count), 'ex...  11.6 us
    select_n x1, local copies, waits for them, and re-layouts, local(): jnp.where(upper_half, section_grads[:, :half_rows], section_grads[:, half...  8.52 us
    all_to_all x1, waiting for transfers between devices, mirror_move(): lax.all_to_all(values, 'pipe', split_axis=split_dim, concat_axis=concat_d...  6.6 us
    all_to_all x1, starting transfers between devices, deliver(): lax.all_to_all(copies, 'expert', split_axis=1, concat_axis=1, tiled=True)  6.55 us
  transfers between devices with their start and end apart: 4, of which 4 were waited for; matrix products, arithmetic and copies ran while one was open for 6% of the time, Pallas kernels for 0%

commit v1 on v0

--- a/solution.py
+++ b/solution.py
@@ -2,9 +2,33 @@
 import jax.numpy as jnp
 from jax import lax
 from jax.sharding import PartitionSpec as P
+from jax.lax import axis_index, axis_size, ppermute
 
 SHARDS = 8
 weight_unit = 0.0625
+
+
+def pass_leaf_by_axis(unit):
+    group_axis = "expert"
+    carry_in, carry_out = (axis_size(group_axis), axis_index(group_axis))
+    current_block = unit.shape[1] // carry_in
+    met_up = list(unit.shape)
+    met_up[1] = current_block
+    t1 = met_up[1]
+    met_up[1] = t1 * carry_in
+    tick = 0
+    everything = jnp.zeros(met_up, unit.dtype)
+    while tick < carry_in:
+        b_next = lax.dynamic_slice_in_dim(
+            unit, (carry_out ^ tick) * current_block, current_block, axis=1
+        )
+        if tick:
+            b_next = ppermute(b_next, group_axis, [(j, j ^ tick) for j in range(carry_in)])
+        everything = lax.dynamic_update_slice_in_dim(
+            everything, b_next, (carry_out ^ tick) * t1, axis=1
+        )
+        tick += 1
+    return everything
 
 
 def hit_tables(routes, mixing, experts, capacity):
@@ -30,7 +54,7 @@
     stacks = slot_rows.shape[0]
     feature_count = slot_rows.shape[2]
     copies = jnp.repeat(slot_rows.reshape(stacks, experts, capacity, feature_count), SHARDS, axis=1)
-    landed = lax.all_to_all(copies, "expert", split_axis=1, concat_axis=1, tiled=True)
+    landed = pass_leaf_by_axis(copies)
     return landed.reshape(stacks, experts * SHARDS * capacity, feature_count)
 
 

time: 314 us -> 344 us (1.096)
  starting transfers between devices: 22.9 us -> 56.5 us
  waiting for transfers between devices: 201 us -> 183 us
  local copies, waits for them, and re-layouts: 41.6 us -> 56.7 us
    all_to_all x1 -> x0, waiting for transfers between devices: 121 us -> none  [deliver(): lax.all_to_all(copies, 'expert', split_axis=1, concat_axis=1, tiled=True)]
    ppermute x0 -> x15, waiting for transfers between devices: none -> 103 us  [pass_leaf_by_axis(): ppermute(b_next, group_axis, [(j, j ^ tick) for j in range(carry_in)])]
    ppermute x0 -> x15, starting transfers between devices: none -> 38.2 us  [pass_leaf_by_axis(): ppermute(b_next, group_axis, [(j, j ^ tick) for j in range(carry_in)])]
    dynamic_update_slice x0 -> x15, local copies, waits for them, and re-layouts: none -> 16.4 us  [pass_leaf_by_axis(): lax.dynamic_update_slice_in_dim(everything, b_next, (carry_out ^ tick) *...]
    all_to_all x1 -> x0, starting transfers between devices: 6.55 us -> none  [deliver(): lax.all_to_all(copies, 'expert', split_axis=1, concat_axis=1, tiled=True)]
  transfers between devices with their start and end apart: 4 -> 18, of which waited for: 4 -> 13; matrix products, arithmetic and copies ran while one was open for 6% -> 9% of each run, Pallas kernels for 0% -> 0%
where the time goes in v1:
time: 344 us; the launch traced here: 343 us
  waiting for transfers between devices  183 us (53%)
  local copies, waits for them, and re-layouts  56.7 us (16%)
  starting transfers between devices  56.5 us (16%)
  blocking collectives  24.3 us (7%)
  matrix products  13.6 us (4%)
  other arithmetic  8.08 us (2%)
    ppermute x15, waiting for transfers between devices, pass_leaf_by_axis(): ppermute(b_next, group_axis, [(j, j ^ tick) for j in range(carry_in)])  103 us
    all_to_all x2, waiting for transfers between devices, collect(): lax.all_to_all(shard_parts.reshape(sources, capacity, feature_count), 'ex...  73.6 us
    ppermute x15, starting transfers between devices, pass_leaf_by_axis(): ppermute(b_next, group_axis, [(j, j ^ tick) for j in range(carry_in)])  38.2 us
    all_to_all x1, blocking collectives, mirror_move(): lax.all_to_all(values, 'pipe', split_axis=split_dim, concat_axis=concat_d...  24.3 us
    dynamic_update_slice x15, local copies, waits for them, and re-layouts, pass_leaf_by_axis(): lax.dynamic_update_slice_in_dim(everything, b_next, (carry_out ^ tick) *...  16.4 us
    all_to_all x2, starting transfers between devices, collect(): lax.all_to_all(shard_parts.reshape(sources, capacity, feature_count), 'ex...  13.7 us
    select_n x1, local copies, waits for them, and re-layouts, local(): jnp.where(upper_half, section_grads[:, :half_rows], section_grads[:, half...  8.54 us
  transfers between devices with their start and end apart: 18, of which 13 were waited for; matrix products, arithmetic and copies ran while one was open for 9% of the time, Pallas kernels for 0%

profile of v1, /device:TPU:13, one launch (start us, length us, event | category | flops | bytes accessed | tf_op | source)
XLA Modules:
  0.0 343.1 jit_solution(3515583153434652443)
XLA Ops:
  2.3 0.8 copy.59
  3.2 0.8 copy.63
  6.5 1.2 convolution_convert_fusion.4
  7.9 1.1 convolution_convert_fusion.6
  9.1 1.1 convolution_convert_fusion.5
  11.8 1.7 constant_dynamic-slice_fusion
  13.6 2.4 copy-done.3
  16.7 1.1 collective-permute-start.14
  17.8 1.1 collective-permute-start.13
  18.9 2.0 collective-permute-start.12
  21.4 1.8 constant_dynamic-update-slice_fusion.13
  23.1 7.7 %collective-permute-done.1 = bf16[3,1,12,3584]{3,2,1,0:T(8,128)(2,1)S(1)} collective-permute-done((bf16[3,1,12,3584]{3,2,1,0:T(8,128)(2,1)}, bf16[3,1,12,3584]{3,2,1,0:T(8,128)(2,1)S(1)}, u32[]{:S(2)}, u32[]{:S(2)}) %collective-permute-start.1) | collective-permute-done | bytes 258080 | tf_op jit(solution)/shard_map/ppermute | solution.py:26
  30.9 1.1 collective-permute-start.2
  32.7 8.9 %collective-permute-done.2 = bf16[3,1,12,3584]{3,2,1,0:T(8,128)(2,1)S(1)} collective-permute-done((bf16[3,1,12,3584]{3,2,1,0:T(8,128)(2,1)}, bf16[3,1,12,3584]{3,2,1,0:T(8,128)(2,1)S(1)}, u32[]{:S(2)}, u32[]{:S(2)}) %collective-permute-start.2) | collective-permute-done | bytes 258080 | tf_op jit(solution)/shard_map/ppermute | solution.py:26
  41.6 13.1 %collective-permute-start.3 = (bf16[3,1,12,3584]{3,2,1,0:T(8,128)(2,1)}, bf16[3,1,12,3584]{3,2,1,0:T(8,128)(2,1)S(1)}, u32[]{:S(2)}, u32[]{:S(2)}) collective-permute-start(bf16[3,1,12,3584]{3,2,1,0:T(8,128)(2,1)} %get-tuple-element.48), channel_id=1, source_target_pairs={{0,4},{1,5},{2,6},{3,7},{4,0},{5,1},{6,2},{7,3},{8,12},{9,13},{10,... | collective-permute-start | bytes 774152 | tf_op jit(solution)/shard_map/ppermute | solution.py:26
  54.6 0.8 constant_dynamic-update-slice_fusion.11
  55.4 7.7 %collective-permute-done.3 = bf16[3,1,12,3584]{3,2,1,0:T(8,128)(2,1)S(1)} collective-permute-done((bf16[3,1,12,3584]{3,2,1,0:T(8,128)(2,1)}, bf16[3,1,12,3584]{3,2,1,0:T(8,128)(2,1)S(1)}, u32[]{:S(2)}, u32[]{:S(2)}) %collective-permute-start.3) | collective-permute-done | bytes 258080 | tf_op jit(solution)/shard_map/ppermute | solution.py:26
  63.1 2.1 collective-permute-start.4
  65.2 0.8 constant_dynamic-update-slice_fusion.10
  66.0 8.2 %collective-permute-done.4 = bf16[3,1,12,3584]{3,2,1,0:T(8,128)(2,1)S(1)} collective-permute-done((bf16[3,1,12,3584]{3,2,1,0:T(8,128)(2,1)}, bf16[3,1,12,3584]{3,2,1,0:T(8,128)(2,1)S(1)}, u32[]{:S(2)}, u32[]{:S(2)}) %collective-permute-start.4) | collective-permute-done | bytes 258080 | tf_op jit(solution)/shard_map/ppermute | solution.py:26
  74.7 0.8 constant_dynamic-update-slice_fusion.9
  75.5 9.2 %collective-permute-done.5 = bf16[3,1,12,3584]{3,2,1,0:T(8,128)(2,1)S(1)} collective-permute-done((bf16[3,1,12,3584]{3,2,1,0:T(8,128)(2,1)S(1)}, bf16[3,1,12,3584]{3,2,1,0:T(8,128)(2,1)S(1)}, u32[]{:S(2)}, u32[]{:S(2)}) %collective-permute-start.5) | collective-permute-done | bytes 258080 | tf_op jit(solution)/shard_map/ppermute | solution.py:26
  84.8 1.3 collective-permute-start.6
  86.0 0.8 constant_dynamic-update-slice_fusion.8
  86.8 9.4 %collective-permute-done.6 = bf16[3,1,12,3584]{3,2,1,0:T(8,128)(2,1)S(1)} collective-permute-done((bf16[3,1,12,3584]{3,2,1,0:T(8,128)(2,1)S(1)}, bf16[3,1,12,3584]{3,2,1,0:T(8,128)(2,1)S(1)}, u32[]{:S(2)}, u32[]{:S(2)}) %collective-permute-start.6) | collective-permute-done | bytes 258080 | tf_op jit(solution)/shard_map/ppermute | solution.py:26
  96.9 0.8 constant_dynamic-update-slice_fusion.7
  97.7 12.6 %collective-permute-done.7 = bf16[3,1,12,3584]{3,2,1,0:T(8,128)(2,1)S(1)} collective-permute-done((bf16[3,1,12,3584]{3,2,1,0:T(8,128)(2,1)S(1)}, bf16[3,1,12,3584]{3,2,1,0:T(8,128)(2,1)S(1)}, u32[]{:S(2)}, u32[]{:S(2)}) %collective-permute-start.7) | collective-permute-done | bytes 258080 | tf_op jit(solution)/shard_map/ppermute | solution.py:26
  110.3 5.3 %collective-permute-start.8 = (bf16[3,1,12,3584]{3,2,1,0:T(8,128)(2,1)S(1)}, bf16[3,1,12,3584]{3,2,1,0:T(8,128)(2,1)S(1)}, u32[]{:S(2)}, u32[]{:S(2)}) collective-permute-start(bf16[3,1,12,3584]{3,2,1,0:T(8,128)(2,1)S(1)} %get-tuple-element.43), channel_id=1, source_target_pairs={{0,9},{1,8},{2,11},{3,10},{4,13},{5,12},{6,15},{7,14},{8,1},{9,0},... | collective-permute-start | bytes 774152 | tf_op jit(solution)/shard_map/ppermute | solution.py:26
  115.6 0.8 constant_dynamic-update-slice_fusion.6
  116.4 12.8 %collective-permute-done.8 = bf16[3,1,12,3584]{3,2,1,0:T(8,128)(2,1)S(1)} collective-permute-done((bf16[3,1,12,3584]{3,2,1,0:T(8,128)(2,1)S(1)}, bf16[3,1,12,3584]{3,2,1,0:T(8,128)(2,1)S(1)}, u32[]{:S(2)}, u32[]{:S(2)}) %collective-permute-start.8) | collective-permute-done | bytes 258080 | tf_op jit(solution)/shard_map/ppermute | solution.py:26
  129.2 4.3 %collective-permute-start.9 = (bf16[3,1,12,3584]{3,2,1,0:T(8,128)(2,1)S(1)}, bf16[3,1,12,3584]{3,2,1,0:T(8,128)(2,1)S(1)}, u32[]{:S(2)}, u32[]{:S(2)}) collective-permute-start(bf16[3,1,12,3584]{3,2,1,0:T(8,128)(2,1)S(1)} %get-tuple-element.42), channel_id=1, source_target_pairs={{0,10},{1,11},{2,8},{3,9},{4,14},{5,15},{6,12},{7,13},{8,2},{9,3},... | collective-permute-start | bytes 774152 | tf_op jit(solution)/shard_map/ppermute | solution.py:26
  133.5 0.8 constant_dynamic-update-slice_fusion.5
  134.3 13.8 %collective-permute-done.9 = bf16[3,1,12,3584]{3,2,1,0:T(8,128)(2,1)S(1)} collective-permute-done((bf16[3,1,12,3584]{3,2,1,0:T(8,128)(2,1)S(1)}, bf16[3,1,12,3584]{3,2,1,0:T(8,128)(2,1)S(1)}, u32[]{:S(2)}, u32[]{:S(2)}) %collective-permute-start.9) | collective-permute-done | bytes 258080 | tf_op jit(solution)/shard_map/ppermute | solution.py:26
  148.1 4.4 %collective-permute-start.10 = (bf16[3,1,12,3584]{3,2,1,0:T(8,128)(2,1)S(1)}, bf16[3,1,12,3584]{3,2,1,0:T(8,128)(2,1)S(1)}, u32[]{:S(2)}, u32[]{:S(2)}) collective-permute-start(bf16[3,1,12,3584]{3,2,1,0:T(8,128)(2,1)S(1)} %get-tuple-element.41), channel_id=1, source_target_pairs={{0,11},{1,10},{2,9},{3,8},{4,15},{5,14},{6,13},{7,12},{8,3},{9,2},... | collective-permute-start | bytes 774152 | tf_op jit(solution)/shard_map/ppermute | solution.py:26
  153.2 12.4 %collective-permute-done.10 = bf16[3,1,12,3584]{3,2,1,0:T(8,128)(2,1)S(1)} collective-permute-done((bf16[3,1,12,3584]{3,2,1,0:T(8,128)(2,1)S(1)}, bf16[3,1,12,3584]{3,2,1,0:T(8,128)(2,1)S(1)}, u32[]{:S(2)}, u32[]{:S(2)}) %collective-permute-start.10) | collective-permute-done | bytes 258080 | tf_op jit(solution)/shard_map/ppermute | solution.py:26
  165.6 0.8 constant_dynamic-update-slice_fusion.3
  166.4 1.7 constant_dynamic-update-slice_fusion.2
  168.1 1.7 constant_dynamic-update-slice_fusion.1
  169.9 1.7 constant_dynamic-update-slice_fusion
  171.6 1.7 constant_dynamic-update-slice_fusion.14
  173.3 4.8 %fusion.38 = (bf16[1,16,12,3584]{3,2,1,0:T(8,128)(2,1)S(1)}, bf16[1,16,12,3584]{3,2,1,0:T(8,128)(2,1)}, bf16[1,16,12,3584]{3,2,1,0:T(8,128)(2,1)}) fusion(bf16[3,16,12,3584]{3,2,1,0:T(8,128)(2,1)} %constant_dynamic-update-slice_fusion.14), kind=kLoop, calls=%fused_computation.101 | loop fusion | bytes 8257536 | tf_op jit(solution)/shard_map/slice | solution.py:126
  178.1 1.3 squeeze.39
  179.4 2.4 squeeze.40
  186.3 8.5 %copy.67 = bf16[3,1792,128]{2,0,1:T(4,128)(2,1)S(1)} copy(bf16[3,1792,128]{2,1,0:T(8,128)(2,1)S(1)} %broadcast_select_fusion) | data formatting | bytes 2752512 | tf_op jit(solution)/shard_map/jit(_where)/select_n | solution.py:158
  194.9 24.3 %all_to_all.34 = bf16[3,1792,128]{2,0,1:T(4,128)(2,1)S(1)} all-to-all(bf16[3,1792,128]{2,0,1:T(4,128)(2,1)S(1)} %copy.67), channel_id=1, replica_groups=mesh['pipe'=2,'expert'=16] {'pipe'}, dimensions={1} | all-to-all | bytes 2752512 | tf_op jit(solution)/shard_map/all_to_all | solution.py:79
  219.3 1.2 reverse.3
  220.5 2.5 copy.69
  223.1 4.6 %all-to-all-start.3 = ((bf16[6,896,128]{2,1,0:T(8,128)(2,1)}), bf16[6,896,128]{2,1,0:T(8,128)(2,1)}, u32[]{:S(2)}, u32[]{:S(2)}) async-start(bf16[6,896,128]{2,1,0:T(8,128)(2,1)} %bitcast.20), calls=%async_computation.3 | async-start | bytes 2752512 | tf_op jit(solution)/shard_map/all_to_all | solution.py:79
  227.7 2.4 squeeze.35
  230.6 3.2 convolution_convert_fusion
  233.8 3.3 reshape.117
  237.1 6.6 %all-to-all-done.3 = bf16[6,896,128]{2,1,0:T(8,128)(2,1)} async-done(((bf16[6,896,128]{2,1,0:T(8,128)(2,1)}), bf16[6,896,128]{2,1,0:T(8,128)(2,1)}, u32[]{:S(2)}, u32[]{:S(2)}) %all-to-all-start.3) | async-done | bytes 1376288 | tf_op jit(solution)/shard_map/all_to_all | solution.py:79
  243.7 8.8 %all-to-all-start = ((bf16[16,12,3584]{2,1,0:T(8,128)(2,1)}), bf16[16,12,3584]{2,1,0:T(8,128)(2,1)}, u32[]{:S(2)}, u32[]{:S(2)}) async-start(bf16[16,12,3584]{2,1,0:T(8,128)(2,1)} %reshape.117), calls=%async_computation | async-start | bytes 3670016 | tf_op jit(solution)/shard_map/all_to_all | solution.py:64
  253.5 1.4 reshape.120
  254.9 39.4 %all-to-all-done = bf16[16,12,3584]{2,1,0:T(8,128)(2,1)} async-done(((bf16[16,12,3584]{2,1,0:T(8,128)(2,1)}), bf16[16,12,3584]{2,1,0:T(8,128)(2,1)}, u32[]{:S(2)}, u32[]{:S(2)}) %all-to-all-start) | async-done | bytes 1376288 | tf_op jit(solution)/shard_map/all_to_all | solution.py:64
  294.3 4.9 %all-to-all-start.1 = ((bf16[16,12,3584]{2,1,0:T(8,128)(2,1)}), bf16[16,12,3584]{2,1,0:T(8,128)(2,1)S(1)}, u32[]{:S(2)}, u32[]{:S(2)}) async-start(bf16[16,12,3584]{2,1,0:T(8,128)(2,1)} %reshape.120), calls=%async_computation.1 | async-start | bytes 3670016 | tf_op jit(solution)/shard_map/all_to_all | solution.py:64
  299.2 1.5 convert_bitcast_fusion
  301.0 1.6 copy-done.2
  303.0 1.0 slice_bitcast_fusion
  304.0 1.0 copy.71
  305.0 1.8 bitcast_reduce_fusion.1
  306.8 34.2 %all-to-all-done.1 = bf16[16,12,3584]{2,1,0:T(8,128)(2,1)S(1)} async-done(((bf16[16,12,3584]{2,1,0:T(8,128)(2,1)}), bf16[16,12,3584]{2,1,0:T(8,128)(2,1)S(1)}, u32[]{:S(2)}, u32[]{:S(2)}) %all-to-all-start.1) | async-done | bytes 1376288 | tf_op jit(solution)/shard_map/all_to_all | solution.py:64
  341.4 0.8 fusion.5
  342.2 0.9 fusion.4
  (74 shorter events, 17.1 us)
Async XLA Ops:
  0.6 181.2 %copy-start = (bf16[1,3584,128]{2,1,0:T(8,128)(2,1)S(1)}, bf16[1,3584,128]{2,1,0:T(8,128)(2,1)}, u32[]{:S(2)}) copy-start(bf16[1,3584,128]{2,1,0:T(8,128)(2,1)} %param.17) | copy-start | bytes 2752516
  13.6 2.4 copy-start.3
  16.0 5.1 %collective-permute-start = (bf16[3,1,12,3584]{3,2,1,0:T(8,128)(2,1)}, bf16[3,1,12,3584]{3,2,1,0:T(8,128)(2,1)}, u32[]{:S(2)}, u32[]{:S(2)}) collective-permute-start(bf16[3,1,12,3584]{3,2,1,0:T(8,128)(2,1)} %get-tuple-element.51), channel_id=1, source_target_pairs={{0,1},{1,0},{2,3},{3,2},{4,5},{5,4},{6,7},{7,6},{8,9},{9,8},{10,11... | collective-permute-start | bytes 774152 | tf_op jit(solution)/shard_map/ppermute | solution.py:26
  16.7 154.9 %collective-permute-start.14 = (bf16[3,1,12,3584]{3,2,1,0:T(8,128)(2,1)S(1)}, bf16[3,1,12,3584]{3,2,1,0:T(8,128)(2,1)}, u32[]{:S(2)}, u32[]{:S(2)}) collective-permute-start(bf16[3,1,12,3584]{3,2,1,0:T(8,128)(2,1)S(1)} %get-tuple-element.37), channel_id=1, source_target_pairs={{0,15},{1,14},{2,13},{3,12},{4,11},{5,10},{6,9},{7,8},{8,7},{9,6},... | collective-permute-start | bytes 774152 | tf_op jit(solution)/shard_map/ppermute | solution.py:26
  17.8 152.1 %collective-permute-start.13 = (bf16[3,1,12,3584]{3,2,1,0:T(8,128)(2,1)S(1)}, bf16[3,1,12,3584]{3,2,1,0:T(8,128)(2,1)}, u32[]{:S(2)}, u32[]{:S(2)}) collective-permute-start(bf16[3,1,12,3584]{3,2,1,0:T(8,128)(2,1)S(1)} %get-tuple-element.38), channel_id=1, source_target_pairs={{0,14},{1,15},{2,12},{3,13},{4,10},{5,11},{6,8},{7,9},{8,6},{9,7},... | collective-permute-start | bytes 774152 | tf_op jit(solution)/shard_map/ppermute | solution.py:26
  18.9 149.2 %collective-permute-start.12 = (bf16[3,1,12,3584]{3,2,1,0:T(8,128)(2,1)S(1)}, bf16[3,1,12,3584]{3,2,1,0:T(8,128)(2,1)}, u32[]{:S(2)}, u32[]{:S(2)}) collective-permute-start(bf16[3,1,12,3584]{3,2,1,0:T(8,128)(2,1)S(1)} %get-tuple-element.39), channel_id=1, source_target_pairs={{0,13},{1,12},{2,15},{3,14},{4,9},{5,8},{6,11},{7,10},{8,5},{9,4},... | collective-permute-start | bytes 774152 | tf_op jit(solution)/shard_map/ppermute | solution.py:26
  20.9 145.5 %collective-permute-start.11 = (bf16[3,1,12,3584]{3,2,1,0:T(8,128)(2,1)S(1)}, bf16[3,1,12,3584]{3,2,1,0:T(8,128)(2,1)}, u32[]{:S(2)}, u32[]{:S(2)}) collective-permute-start(bf16[3,1,12,3584]{3,2,1,0:T(8,128)(2,1)S(1)} %get-tuple-element.40), channel_id=1, source_target_pairs={{0,12},{1,13},{2,14},{3,15},{4,8},{5,9},{6,10},{7,11},{8,4},{9,5},... | collective-permute-start | bytes 774152 | tf_op jit(solution)/shard_map/ppermute | solution.py:26
  21.1 53.1 %copy-start.9 = (bf16[3,1,12,3584]{3,2,1,0:T(8,128)(2,1)S(1)}, bf16[3,1,12,3584]{3,2,1,0:T(8,128)(2,1)}, u32[]{:S(2)}) copy-start(bf16[3,1,12,3584]{3,2,1,0:T(8,128)(2,1)} %get-tuple-element.46) | copy-start | bytes 774148
  21.1 63.7 %copy-start.8 = (bf16[3,1,12,3584]{3,2,1,0:T(8,128)(2,1)S(1)}, bf16[3,1,12,3584]{3,2,1,0:T(8,128)(2,1)}, u32[]{:S(2)}) copy-start(bf16[3,1,12,3584]{3,2,1,0:T(8,128)(2,1)} %get-tuple-element.45) | copy-start | bytes 774148
  21.1 75.2 %copy-start.7 = (bf16[3,1,12,3584]{3,2,1,0:T(8,128)(2,1)S(1)}, bf16[3,1,12,3584]{3,2,1,0:T(8,128)(2,1)}, u32[]{:S(2)}) copy-start(bf16[3,1,12,3584]{3,2,1,0:T(8,128)(2,1)} %get-tuple-element.44) | copy-start | bytes 774148
  21.1 9.8 %collective-permute-start.1 = (bf16[3,1,12,3584]{3,2,1,0:T(8,128)(2,1)}, bf16[3,1,12,3584]{3,2,1,0:T(8,128)(2,1)S(1)}, u32[]{:S(2)}, u32[]{:S(2)}) collective-permute-start(bf16[3,1,12,3584]{3,2,1,0:T(8,128)(2,1)} %get-tuple-element.50), channel_id=1, source_target_pairs={{0,2},{1,3},{2,0},{3,1},{4,6},{5,7},{6,4},{7,5},{8,10},{9,11},{10,... | collective-permute-start | bytes 774152 | tf_op jit(solution)/shard_map/ppermute | solution.py:26
  30.9 10.7 %collective-permute-start.2 = (bf16[3,1,12,3584]{3,2,1,0:T(8,128)(2,1)}, bf16[3,1,12,3584]{3,2,1,0:T(8,128)(2,1)S(1)}, u32[]{:S(2)}, u32[]{:S(2)}) collective-permute-start(bf16[3,1,12,3584]{3,2,1,0:T(8,128)(2,1)} %get-tuple-element.49), channel_id=1, source_target_pairs={{0,3},{1,2},{2,1},{3,0},{4,7},{5,6},{6,5},{7,4},{8,11},{9,10},{10,... | collective-permute-start | bytes 774152 | tf_op jit(solution)/shard_map/ppermute | solution.py:26
  41.6 21.5 %collective-permute-start.3 = (bf16[3,1,12,3584]{3,2,1,0:T(8,128)(2,1)}, bf16[3,1,12,3584]{3,2,1,0:T(8,128)(2,1)S(1)}, u32[]{:S(2)}, u32[]{:S(2)}) collective-permute-start(bf16[3,1,12,3584]{3,2,1,0:T(8,128)(2,1)} %get-tuple-element.48), channel_id=1, source_target_pairs={{0,4},{1,5},{2,6},{3,7},{4,0},{5,1},{6,2},{7,3},{8,12},{9,13},{10,... | collective-permute-start | bytes 774152 | tf_op jit(solution)/shard_map/ppermute | solution.py:26
  63.1 11.1 %collective-permute-start.4 = (bf16[3,1,12,3584]{3,2,1,0:T(8,128)(2,1)}, bf16[3,1,12,3584]{3,2,1,0:T(8,128)(2,1)S(1)}, u32[]{:S(2)}, u32[]{:S(2)}) collective-permute-start(bf16[3,1,12,3584]{3,2,1,0:T(8,128)(2,1)} %get-tuple-element.47), channel_id=1, source_target_pairs={{0,5},{1,4},{2,7},{3,6},{4,1},{5,0},{6,3},{7,2},{8,13},{9,12},{10,... | collective-permute-start | bytes 774152 | tf_op jit(solution)/shard_map/ppermute | solution.py:26
  74.2 10.6 %collective-permute-start.5 = (bf16[3,1,12,3584]{3,2,1,0:T(8,128)(2,1)S(1)}, bf16[3,1,12,3584]{3,2,1,0:T(8,128)(2,1)S(1)}, u32[]{:S(2)}, u32[]{:S(2)}) collective-permute-start(bf16[3,1,12,3584]{3,2,1,0:T(8,128)(2,1)S(1)} %copy-done.9), channel_id=1, source_target_pairs={{0,6},{1,7},{2,4},{3,5},{4,2},{5,3},{6,0},{7,1},{8,14},{9,15},{10,... | collective-permute-start | bytes 774152 | tf_op jit(solution)/shard_map/ppermute | solution.py:26
  84.8 11.5 %collective-permute-start.6 = (bf16[3,1,12,3584]{3,2,1,0:T(8,128)(2,1)S(1)}, bf16[3,1,12,3584]{3,2,1,0:T(8,128)(2,1)S(1)}, u32[]{:S(2)}, u32[]{:S(2)}) collective-permute-start(bf16[3,1,12,3584]{3,2,1,0:T(8,128)(2,1)S(1)} %copy-done.8), channel_id=1, source_target_pairs={{0,7},{1,6},{2,5},{3,4},{4,3},{5,2},{6,1},{7,0},{8,15},{9,14},{10,... | collective-permute-start | bytes 774152 | tf_op jit(solution)/shard_map/ppermute | solution.py:26
  96.2 14.1 %collective-permute-start.7 = (bf16[3,1,12,3584]{3,2,1,0:T(8,128)(2,1)S(1)}, bf16[3,1,12,3584]{3,2,1,0:T(8,128)(2,1)S(1)}, u32[]{:S(2)}, u32[]{:S(2)}) collective-permute-start(bf16[3,1,12,3584]{3,2,1,0:T(8,128)(2,1)S(1)} %copy-done.7), channel_id=1, source_target_pairs={{0,8},{1,9},{2,10},{3,11},{4,12},{5,13},{6,14},{7,15},{8,0},{9,1},... | collective-permute-start | bytes 774152 | tf_op jit(solution)/shard_map/ppermute | solution.py:26
  110.3 18.9 %collective-permute-start.8 = (bf16[3,1,12,3584]{3,2,1,0:T(8,128)(2,1)S(1)}, bf16[3,1,12,3584]{3,2,1,0:T(8,128)(2,1)S(1)}, u32[]{:S(2)}, u32[]{:S(2)}) collective-permute-start(bf16[3,1,12,3584]{3,2,1,0:T(8,128)(2,1)S(1)} %get-tuple-element.43), channel_id=1, source_target_pairs={{0,9},{1,8},{2,11},{3,10},{4,13},{5,12},{6,15},{7,14},{8,1},{9,0},... | collective-permute-start | bytes 774152 | tf_op jit(solution)/shard_map/ppermute | solution.py:26
  129.2 18.9 %collective-permute-start.9 = (bf16[3,1,12,3584]{3,2,1,0:T(8,128)(2,1)S(1)}, bf16[3,1,12,3584]{3,2,1,0:T(8,128)(2,1)S(1)}, u32[]{:S(2)}, u32[]{:S(2)}) collective-permute-start(bf16[3,1,12,3584]{3,2,1,0:T(8,128)(2,1)S(1)} %get-tuple-element.42), channel_id=1, source_target_pairs={{0,10},{1,11},{2,8},{3,9},{4,14},{5,15},{6,12},{7,13},{8,2},{9,3},... | collective-permute-start | bytes 774152 | tf_op jit(solution)/shard_map/ppermute | solution.py:26
  148.1 17.5 %collective-permute-start.10 = (bf16[3,1,12,3584]{3,2,1,0:T(8,128)(2,1)S(1)}, bf16[3,1,12,3584]{3,2,1,0:T(8,128)(2,1)S(1)}, u32[]{:S(2)}, u32[]{:S(2)}) collective-permute-start(bf16[3,1,12,3584]{3,2,1,0:T(8,128)(2,1)S(1)} %get-tuple-element.41), channel_id=1, source_target_pairs={{0,11},{1,10},{2,9},{3,8},{4,15},{5,14},{6,13},{7,12},{8,3},{9,2},... | collective-permute-start | bytes 774152 | tf_op jit(solution)/shard_map/ppermute | solution.py:26
  179.4 3.0 copy-start.4
  181.8 1.3 copy-start.5
  182.4 1.5 copy-start.6
  186.1 8.7 %copy-start.1 = (bf16[3,3584,128]{2,1,0:T(8,128)(2,1)}, bf16[3,3584,128]{2,1,0:T(8,128)(2,1)S(1)}, u32[]{:S(2)}) copy-start(bf16[3,3584,128]{2,1,0:T(8,128)(2,1)S(1)} %pad_maximum_fusion) | copy-start | bytes 8257540
  223.1 20.6 %all-to-all-start.3 = ((bf16[6,896,128]{2,1,0:T(8,128)(2,1)}), bf16[6,896,128]{2,1,0:T(8,128)(2,1)}, u32[]{:S(2)}, u32[]{:S(2)}) async-start(bf16[6,896,128]{2,1,0:T(8,128)(2,1)} %bitcast.20), calls=%async_computation.3 | async-start | bytes 2752512 | tf_op jit(solution)/shard_map/all_to_all | solution.py:79
  243.7 50.7 %all-to-all-start = ((bf16[16,12,3584]{2,1,0:T(8,128)(2,1)}), bf16[16,12,3584]{2,1,0:T(8,128)(2,1)}, u32[]{:S(2)}, u32[]{:S(2)}) async-start(bf16[16,12,3584]{2,1,0:T(8,128)(2,1)} %reshape.117), calls=%async_computation | async-start | bytes 3670016 | tf_op jit(solution)/shard_map/all_to_all | solution.py:64
  294.3 46.7 %all-to-all-start.1 = ((bf16[16,12,3584]{2,1,0:T(8,128)(2,1)}), bf16[16,12,3584]{2,1,0:T(8,128)(2,1)S(1)}, u32[]{:S(2)}, u32[]{:S(2)}) async-start(bf16[16,12,3584]{2,1,0:T(8,128)(2,1)} %reshape.120), calls=%async_computation.1 | async-start | bytes 3670016 | tf_op jit(solution)/shard_map/all_to_all | solution.py:64
  300.8 1.8 copy-start.2
